TPU v7x, 32 devices: a whole 2x2x4 slice. The times are simulated.
32 devices in a mesh: dp: 8 (over y, x, core), tensor: 4 (over z).
Axes of the slice: x: 2, y: 2, z: 4, core: 2. Of those that a mesh axis runs over, the one named last changes fastest.
Arguments:
- block_input: bfloat16 [4096, 1024], P('dp'), may hold values from -6 to 6
- cotangent: bfloat16 [4096, 1024], P('dp'), may hold values from -6 to 6
- seq_lengths: int32 [8, 4], P('dp'), may hold values from 0 to 512, as said below
- norm_gains: float32 [2, 2, 1024], replicated, may hold values from 0.1 to 1.9
- norm_biases: float32 [2, 2, 1024], replicated, may hold values from -3 to 3
- w_qkv: bfloat16 [2, 1024, 3, 1024], P(None, None, None, 'tensor'), may hold values from -0.1875 to 0.1875
- qv_bias: float32 [2, 2, 1024], P(None, None, 'tensor'), may hold values from -3 to 3
- w_out: bfloat16 [2, 1024, 1024], P(None, 'tensor'), may hold values from -0.375 to 0.375
- out_biases: float32 [2, 2, 1024], replicated, may hold values from -3 to 3
- w_up: bfloat16 [2, 1024, 4096], P(None, None, 'tensor'), may hold values from -0.1875 to 0.1875
- up_bias: float32 [2, 4096], P(None, 'tensor'), may hold values from -3 to 3
- w_down: bfloat16 [2, 4096, 1024], P(None, 'tensor'), may hold values from -0.09375 to 0.09375
Outputs:
- block_output: bfloat16 [4096, 1024], P('dp')
- input_grad: float32 [4096, 1024], P('dp')
- grad_norm_gains: float32 [2, 2, 1024], replicated
- grad_norm_biases: float32 [2, 2, 1024], replicated
- grad_w_qkv: float32 [2, 1024, 3, 1024], P(None, 'dp', None, 'tensor')
- grad_qv_bias: float32 [2, 2, 1024], P(None, None, 'tensor')
- grad_w_out: float32 [2, 1024, 1024], P(None, 'tensor', 'dp')
- grad_out_biases: float32 [2, 2, 1024], replicated
- grad_w_up: float32 [2, 1024, 4096], P(None, 'dp', 'tensor')
- grad_up_bias: float32 [2, 4096], P(None, 'tensor')
- grad_w_down: float32 [2, 4096, 1024], P(None, 'tensor', 'dp')
Inputs may be any that keep to these rules, and one draw needn't show every extreme that they name: `seq_lengths`: each row's lengths sum to at most 512; zero lengths occur; in every draw one row holds a single sequence of exactly 512 tokens.
All inputs are finite; a program needn't handle non-finite values.
Results may differ from a plain program's by a relative error of at most 0.025.
Values may be sent and summed in bfloat16 or wider, within the bound.
A program may use at most 128 MiB of HBM per device.

v0:
```python
import jax
import jax.numpy as jnp
from jax import lax
from jax.sharding import PartitionSpec as P

HEADS = 16
HEAD_DIM = 64
NORM_EPS = 1e-05


def layer_norm(residual, gain_vec, shift_vec):
    mean_row = jnp.mean(residual, axis=-1, keepdims=True)
    centered = residual - mean_row
    variance = jnp.mean(centered * centered, axis=-1, keepdims=True)
    return centered * lax.rsqrt(variance + NORM_EPS) * gain_vec + shift_vec


def gelu_tanh(pre_act):
    return (
        0.5
        * pre_act
        * (1.0 + jnp.tanh(0.7978845608028654 * (pre_act + 0.044715 * pre_act * pre_act * pre_act)))
    )


def norm_back(residual, gain_vec, shift_vec, grad_normed):
    result, pull_back = jax.vjp(layer_norm, residual, gain_vec, shift_vec)
    return pull_back(grad_normed)


def segment_mask(lengths, row_count):
    seq_ends = jnp.cumsum(lengths)
    position = jnp.arange(row_count, dtype=jnp.int32)
    segment = jnp.sum((position[:, None] >= seq_ends[None, :]).astype(jnp.int32), axis=1)
    same_seq = (segment[:, None] == segment[None, :]) & (position[None, :] <= position[:, None])
    row_gap = (position[:, None] - position[None, :]).astype(jnp.float32)
    live_rows = (position < seq_ends[-1]).astype(jnp.float32)
    return (same_seq, row_gap, live_rows)


def on_device(
    block_input,
    cotangent,
    seq_lengths,
    norm_gains,
    norm_biases,
    w_qkv,
    qv_bias,
    w_out,
    out_biases,
    w_up,
    up_bias,
    w_down,
):
    row_count = block_input.shape[0]
    my_rank = lax.axis_index("tensor")
    local_width = w_qkv.shape[3]
    heads_here = local_width // HEAD_DIM
    depth = w_qkv.shape[0]
    score_scale = HEAD_DIM ** (-0.5)
    f32 = jnp.float32
    same_seq, row_gap, live_rows = segment_mask(seq_lengths[0], row_count)
    head_index = my_rank * heads_here + jnp.arange(heads_here, dtype=jnp.int32) + 1
    slopes = jnp.exp2(-8.0 * head_index.astype(f32) / HEADS)

    def branch_total(partial_value):
        return lax.psum(partial_value.astype(jnp.bfloat16), "tensor").astype(jnp.float32)

    def input_total(partial_value):
        return lax.psum(partial_value.astype(jnp.bfloat16), "tensor").astype(jnp.float32)

    def score_block(queries, key_rows):
        raw_scores = (
            jnp.einsum("the,she->hts", queries, key_rows, preferred_element_type=f32) * score_scale
        )
        raw_scores = raw_scores - slopes[:, None, None] * row_gap
        return jnp.where(same_seq, raw_scores, -1000000000.0)

    head_shape = (row_count, heads_here, HEAD_DIM)
    residual = block_input.astype(f32)
    stored = []
    for layer_idx in range(depth):
        entering = residual
        normed = layer_norm(residual, norm_gains[layer_idx, 0], norm_biases[layer_idx, 0]).astype(
            jnp.bfloat16
        )
        projected = jnp.einsum("td,dcn->tcn", normed, w_qkv[layer_idx], preferred_element_type=f32)
        queries = (projected[:, 0] + qv_bias[layer_idx, 0]).astype(jnp.bfloat16).reshape(head_shape)
        key_rows = projected[:, 1].astype(jnp.bfloat16).reshape(head_shape)
        value_rows = (
            (projected[:, 2] + qv_bias[layer_idx, 1]).astype(jnp.bfloat16).reshape(head_shape)
        )
        scores = score_block(queries, key_rows)
        row_max = jnp.max(scores, axis=-1, keepdims=True)
        log_total = row_max + jnp.log(jnp.sum(jnp.exp(scores - row_max), axis=-1, keepdims=True))
        softmax_p = jnp.exp(scores - log_total).astype(jnp.bfloat16)
        context = jnp.einsum("hts,she->the", softmax_p, value_rows, preferred_element_type=f32)
        context = context.astype(jnp.bfloat16).reshape(row_count, local_width)
        partial_value = jnp.dot(context, w_out[layer_idx], preferred_element_type=f32)
        residual = residual + branch_total(partial_value) + out_biases[layer_idx, 0]
        middle = residual
        normed_mlp = layer_norm(
            residual, norm_gains[layer_idx, 1], norm_biases[layer_idx, 1]
        ).astype(jnp.bfloat16)
        up_proj = (
            jnp.dot(normed_mlp, w_up[layer_idx], preferred_element_type=f32) + up_bias[layer_idx]
        )
        activated = gelu_tanh(up_proj).astype(jnp.bfloat16)
        partial_value = jnp.dot(activated, w_down[layer_idx], preferred_element_type=f32)
        residual = residual + branch_total(partial_value) + out_biases[layer_idx, 1]
        stored.append(
            (
                entering,
                normed,
                queries,
                key_rows,
                value_rows,
                log_total,
                context,
                middle,
                normed_mlp,
                up_proj,
                activated,
            )
        )
    block_rows = residual.astype(jnp.bfloat16)
    grad_rows = cotangent.astype(f32) * live_rows[:, None]
    small_parts = []
    heavy_parts = []
    for layer_idx in reversed(range(depth)):
        (
            entering,
            normed,
            queries,
            key_rows,
            value_rows,
            log_total,
            context,
            middle,
            normed_mlp,
            up_proj,
            activated,
        ) = stored[layer_idx]
        down_bias_grad = jnp.sum(grad_rows, axis=0)
        grad_low = grad_rows.astype(jnp.bfloat16)
        down_w_grad = jnp.einsum("tf,td->fd", activated, grad_low, preferred_element_type=f32)
        act_grad = jnp.einsum("td,fd->tf", grad_low, w_down[layer_idx], preferred_element_type=f32)
        up_grad = jax.vjp(gelu_tanh, up_proj)[1](act_grad)[0].astype(jnp.bfloat16)
        up_bias_grad = jnp.sum(up_grad.astype(f32), axis=0)
        up_w_grad = jnp.einsum("td,tf->df", normed_mlp, up_grad, preferred_element_type=f32)
        normed_grad = input_total(
            jnp.einsum("tf,df->td", up_grad, w_up[layer_idx], preferred_element_type=f32)
        )
        middle_grad, gain_mlp, shift_mlp = norm_back(
            middle, norm_gains[layer_idx, 1], norm_biases[layer_idx, 1], normed_grad
        )
        grad_rows = grad_rows + middle_grad
        out_bias_grad = jnp.sum(grad_rows, axis=0)
        grad_low = grad_rows.astype(jnp.bfloat16)
        out_w_grad = jnp.einsum("tn,td->nd", context, grad_low, preferred_element_type=f32)
        context_grad = jnp.einsum(
            "td,nd->tn", grad_low, w_out[layer_idx], preferred_element_type=f32
        )
        context_grad = context_grad.astype(jnp.bfloat16).reshape(head_shape)
        scores = score_block(queries, key_rows)
        softmax_f = jnp.exp(scores - log_total)
        prob_grad = jnp.einsum("the,she->hts", context_grad, value_rows, preferred_element_type=f32)
        score_grad = softmax_f * (
            prob_grad - jnp.sum(prob_grad * softmax_f, axis=-1, keepdims=True)
        )
        score_grad = score_grad.astype(jnp.bfloat16)
        query_grad = (
            jnp.einsum("hts,she->the", score_grad, key_rows, preferred_element_type=f32)
            * score_scale
        )
        key_grad = (
            jnp.einsum("hts,the->she", score_grad, queries, preferred_element_type=f32)
            * score_scale
        )
        value_grad = jnp.einsum(
            "hts,the->she", softmax_f.astype(jnp.bfloat16), context_grad, preferred_element_type=f32
        )
        qkv_grad = (
            jnp.stack([query_grad, key_grad, value_grad], axis=1)
            .astype(jnp.bfloat16)
            .reshape(row_count, 3, local_width)
        )
        qkv_w_grad = jnp.einsum("td,tcn->dcn", normed, qkv_grad, preferred_element_type=f32)
        qv_bias_grad = jnp.sum(qkv_grad[:, 0::2].astype(f32), axis=0)
        normed_grad = input_total(
            jnp.einsum("tcn,dcn->td", qkv_grad, w_qkv[layer_idx], preferred_element_type=f32)
        )
        enter_grad, gain_attn, shift_attn = norm_back(
            entering, norm_gains[layer_idx, 0], norm_biases[layer_idx, 0], normed_grad
        )
        grad_rows = grad_rows + enter_grad
        small_parts.append(
            (
                jnp.stack([gain_attn, gain_mlp]),
                jnp.stack([shift_attn, shift_mlp]),
                jnp.stack([out_bias_grad, down_bias_grad]),
                qv_bias_grad,
                up_bias_grad,
            )
        )
        heavy = (qkv_w_grad, out_w_grad, up_w_grad, down_w_grad)
        heavy_parts.append(heavy)
    small_parts = small_parts[::-1]
    heavy_parts = heavy_parts[::-1]
    gain_grads = jnp.stack([entry[0] for entry in small_parts])
    shift_grads = jnp.stack([entry[1] for entry in small_parts])
    bias_grads = jnp.stack([entry[2] for entry in small_parts])
    qv_grads = jnp.stack([entry[3] for entry in small_parts])
    up_bias_grads = jnp.stack([entry[4] for entry in small_parts])
    gain_grads, shift_grads, bias_grads = (gain_grads, shift_grads, bias_grads)
    gain_grads, shift_grads, bias_grads, qv_grads, up_bias_grads = (
        lax.psum(gain_grads.astype(jnp.bfloat16), "dp").astype(jnp.float32),
        lax.psum(shift_grads.astype(jnp.bfloat16), "dp").astype(jnp.float32),
        lax.psum(bias_grads.astype(jnp.bfloat16), "dp").astype(jnp.float32),
        lax.psum(qv_grads.astype(jnp.bfloat16), "dp").astype(jnp.float32),
        lax.psum(up_bias_grads.astype(jnp.bfloat16), "dp").astype(jnp.float32),
    )
    qkv_all = jnp.stack([entry[0] for entry in heavy_parts])
    out_all = jnp.stack([entry[1] for entry in heavy_parts])
    up_all = jnp.stack([entry[2] for entry in heavy_parts])
    down_all = jnp.stack([entry[3] for entry in heavy_parts])
    qkv_all, out_all, up_all, down_all = (
        lax.psum_scatter(
            qkv_all.astype(jnp.bfloat16), "dp", scatter_dimension=1, tiled=True
        ).astype(jnp.float32),
        lax.psum_scatter(
            out_all.astype(jnp.bfloat16), "dp", scatter_dimension=2, tiled=True
        ).astype(jnp.float32),
        lax.psum_scatter(up_all.astype(jnp.bfloat16), "dp", scatter_dimension=1, tiled=True).astype(
            jnp.float32
        ),
        lax.psum_scatter(
            down_all.astype(jnp.bfloat16), "dp", scatter_dimension=2, tiled=True
        ).astype(jnp.float32),
    )
    return (
        block_rows,
        grad_rows,
        gain_grads,
        shift_grads,
        qkv_all,
        qv_grads,
        out_all,
        bias_grads,
        up_all,
        up_bias_grads,
        down_all,
    )


def solution(mesh):
    in_specs = (
        P("dp", None),
        P("dp", None),
        P("dp", None),
        P(),
        P(),
        P(None, None, None, "tensor"),
        P(None, None, "tensor"),
        P(None, "tensor", None),
        P(),
        P(None, None, "tensor"),
        P(None, "tensor"),
        P(None, "tensor", None),
    )
    out_specs = (
        P("dp", None),
        P("dp", None),
        P(),
        P(),
        P(None, "dp", None, "tensor"),
        P(None, None, "tensor"),
        P(None, "tensor", "dp"),
        P(),
        P(None, "dp", "tensor"),
        P(None, "tensor"),
        P(None, "tensor", "dp"),
    )
    return jax.shard_map(
        on_device, mesh=mesh, in_specs=in_specs, out_specs=out_specs, check_vma=False
    )
```

profile of v0, /device:TPU:0, one launch (start us, length us, event | category | flops | bytes accessed | tf_op | source)
XLA Modules:
  0.0 713.0 jit_solution(7808958398125200820)
XLA Ops:
  24.6 54.7 %all-reduce.10.cloned.1.call-done = bf16[512,1024]{1,0:T(8,128)(2,1)} async-done(((bf16[512,1024]{1,0:T(8,128)(2,1)}), bf16[512,1024]{1,0:T(8,128)(2,1)}) %all-reduce.10.cloned.1.call-update) | async-done | bytes 1048592 | tf_op jit(solution)/shard_map/psum | solution.py:67
  89.1 51.0 %all-reduce.12.cloned.1.call-done = bf16[512,1024]{1,0:T(8,128)(2,1)} async-done(((bf16[512,1024]{1,0:T(8,128)(2,1)}), bf16[512,1024]{1,0:T(8,128)(2,1)}) %all-reduce.12.cloned.1.call-update) | async-done | bytes 1048592 | tf_op jit(solution)/shard_map/psum | solution.py:67
  153.1 50.0 %all-reduce.14.cloned.1.call-done = bf16[512,1024]{1,0:T(8,128)(2,1)} async-done(((bf16[512,1024]{1,0:T(8,128)(2,1)}), bf16[512,1024]{1,0:T(8,128)(2,1)}) %all-reduce.14.cloned.1.call-update) | async-done | bytes 1048592 | tf_op jit(solution)/shard_map/psum | solution.py:67
  209.3 3.4 fusion.155
  216.5 50.8 %all-reduce.16.cloned.1.call-done = bf16[512,1024]{1,0:T(8,128)(2,1)} async-done(((bf16[512,1024]{1,0:T(8,128)(2,1)}), bf16[512,1024]{1,0:T(8,128)(2,1)}) %all-reduce.16.cloned.1.call-update) | async-done | bytes 1048592 | tf_op jit(solution)/shard_map/psum | solution.py:70
  285.5 3.6 bitcast_convert_fusion.1
  289.4 51.1 %all-reduce.18.cloned.1.call-done = bf16[512,1024]{1,0:T(8,128)(2,1)} async-done(((bf16[512,1024]{1,0:T(8,128)(2,1)}), bf16[512,1024]{1,0:T(8,128)(2,1)}) %all-reduce.18.cloned.1.call-update) | async-done | bytes 1048592 | tf_op jit(solution)/shard_map/psum | solution.py:70
  348.3 3.6 fusion.156
  355.3 4.8 fusion.83
  361.4 45.2 %all-reduce.20.cloned.1.call-done = bf16[512,1024]{1,0:T(8,128)(2,1)} async-done(((bf16[512,1024]{1,0:T(8,128)(2,1)}), bf16[512,1024]{1,0:T(8,128)(2,1)}) %all-reduce.20.cloned.1.call-update) | async-done | bytes 1048592 | tf_op jit(solution)/shard_map/psum | solution.py:70
  415.7 3.7 copy.97
  422.1 3.6 multiply_reduce_fusion
  431.2 3.3 fusion.102
  436.3 3.7 convolution_convert_fusion.6
  441.7 3.6 bitcast_convert_fusion
  452.9 3.8 convert_bitcast_fusion
  460.7 11.4 %copy.99 = bf16[2,1024,1024]{1,0,2:T(2,128)(2,1)} copy(bf16[2,1024,1024]{2,1,0:T(8,128)(2,1)} %pad_maximum_fusion.1) | data formatting | bytes 8388608
  472.1 5.6 copy.104
  494.0 52.3 %all-reduce.22.cloned.1.call-done = (bf16[512,1024]{1,0:T(8,128)(2,1)}, bf16[512,1024]{1,0:T(8,128)(2,1)}) async-done(((bf16[512,1024]{1,0:T(8,128)(2,1)}, bf16[512,1024]{1,0:T(8,128)(2,1)}), (bf16[512,1024]{1,0:T(8,128)(2,1)}, bf16[512,1024]{1,0:T(8,128)(2,1)})) %all-reduce.22.cloned.1.call-update) | async-done | bytes 2097168 | tf_op jit(solution)/shard_map/psum | solution.py:67
  551.0 24.5 %all-reduce = (bf16[2,2,1024]{2,1,0:T(2,128)(2,1)S(1)}, bf16[2,2,1024]{2,1,0:T(2,128)(2,1)S(1)}, bf16[2,2,256]{2,1,0:T(2,128)(2,1)S(1)}, bf16[2,2,1024]{2,1,0:T(2,128)(2,1)S(1)}, bf16[2,1024]{1,0:T(2,128)(2,1)S(1)}) all-reduce(bf16[2,2,1024]{2,1,0:T(2,128)(2,1)S(1)} %pad_maximum_fusion.6, ...), channel_id=1, replica_groups=mesh['dp'=8,'tensor'=4] {'dp'}, use_global_device_ids=true, to_apply=%region_36.37 | all-reduce | flops 15360 | bytes 61440 | tf_op jit(solution)/shard_map/psum | solution.py:217
  578.5 4.6 add_add_fusion.4
  583.2 11.8 %reduce-scatter.9.cloned.1.call-done = bf16[2,128,3,256]{3,1,2,0:T(8,128)(2,1)} async-done(((bf16[2,1024,3,256]{3,1,2,0:T(8,128)(2,1)}), bf16[2,128,3,256]{3,1,2,0:T(8,128)(2,1)}) %reduce-scatter.9.cloned.1.call-update) | async-done | bytes 393232 | tf_op jit(solution)/shard_map/reduce_scatter | solution.py:228
  596.9 52.4 %reduce-scatter.15.cloned.1.call-done = bf16[128,2048]{1,0:T(8,128)(2,1)} async-done(((bf16[1024,2048]{1,0:T(8,128)(2,1)}), bf16[128,2048]{1,0:T(8,128)(2,1)}) %reduce-scatter.15.cloned.1.call-update) | async-done | bytes 524304
  652.3 51.5 %reduce-scatter.11.cloned.1.call-done = bf16[2,128,1024]{2,1,0:T(8,128)(2,1)} async-done(((bf16[2,1024,1024]{2,1,0:T(8,128)(2,1)}), bf16[2,128,1024]{2,1,0:T(8,128)(2,1)}) %reduce-scatter.11.cloned.1.call-update) | async-done | bytes 524304 | tf_op jit(solution)/shard_map/reduce_scatter | solution.py:234
  (307 shorter events, 143.5 us)
Async XLA Ops:
  7.2 72.1 %all-reduce.10.cloned.1.call-start = ((), (), s32[]{:S(2)}) async-start(), calls=%async_computation.4 | async-start | bytes 2097152 | tf_op jit(solution)/shard_map/psum | solution.py:67
  13.2 4.7 copy-start.31
  13.2 6.7 copy-start.22
  13.3 4.6 copy-start.35
  24.5 115.5 %all-reduce.12.cloned.1.call-start = ((), (), s32[]{:S(2)}) async-start(), calls=%async_computation.5 | async-start | bytes 2097152 | tf_op jit(solution)/shard_map/psum | solution.py:67
  81.6 4.5 copy-start.59
  88.6 114.5 %all-reduce.14.cloned.1.call-start = ((), (), s32[]{:S(2)}) async-start(), calls=%async_computation.6 | async-start | bytes 2097152 | tf_op jit(solution)/shard_map/psum | solution.py:67
  144.1 3.8 copy-start.23
  149.9 53.2 %copy-start.29 = (bf16[4,64,512]{2,1,0:T(8,128)(2,1)}, bf16[4,64,512]{2,1,0:T(8,128)(2,1)S(1)}, u32[]{:S(2)}) copy-start(bf16[4,64,512]{2,1,0:T(8,128)(2,1)S(1)} %convolution_convert_fusion.10) | copy-start | bytes 786436
  151.9 115.5 %all-reduce.16.cloned.1.call-start = ((), (), s32[]{:S(2)}) async-start(), calls=%async_computation.7 | async-start | bytes 2097152 | tf_op jit(solution)/shard_map/psum | solution.py:70
  207.6 5.1 copy-start.68
  216.0 124.5 %all-reduce.18.cloned.1.call-start = ((), (), s32[]{:S(2)}) async-start(), calls=%async_computation.8 | async-start | bytes 2097152 | tf_op jit(solution)/shard_map/psum | solution.py:70
  289.2 117.4 %all-reduce.20.cloned.1.call-start = ((), (), s32[]{:S(2)}) async-start(), calls=%async_computation.9 | async-start | bytes 2097152 | tf_op jit(solution)/shard_map/psum | solution.py:70
  345.5 6.5 copy-start.19
  348.3 4.6 copy-start.58
  355.2 137.0 %reduce-scatter.13.cloned.1.call-start = ((), (), s32[]{:S(2)}) async-start(), calls=%async_computation.12 | async-start | bytes 1179648
  355.3 4.9 copy-start.12
  355.3 4.9 copy-start.30
  421.8 124.6 %all-reduce.22.cloned.1.call-start = ((), (), s32[]{:S(2)}) async-start(), calls=%async_computation.14 | async-start | bytes 4194304 | tf_op jit(solution)/shard_map/psum | solution.py:67
  445.3 149.6 %reduce-scatter.9.cloned.1.call-start = ((), (), s32[]{:S(2)}) async-start(), calls=%async_computation.10 | async-start | bytes 3538944 | tf_op jit(solution)/shard_map/reduce_scatter | solution.py:228
  452.6 196.7 %reduce-scatter.15.cloned.1.call-start = ((), (), s32[]{:S(2)}) async-start(), calls=%async_computation.13 | async-start | bytes 4718592
  452.9 3.9 copy-start.21
  452.9 3.9 copy-start.66
  477.7 226.1 %reduce-scatter.11.cloned.1.call-start = ((), (), s32[]{:S(2)}) async-start(), calls=%async_computation.11 | async-start | bytes 4718592 | tf_op jit(solution)/shard_map/reduce_scatter | solution.py:234
  (58 other events, 126.5 us)
Sparse Core Ops, SparseCore 0:
  24.6 54.6 all-reduce.9
  88.7 51.2 all-reduce.11
  152.0 51.1 all-reduce.13
  216.1 51.1 all-reduce.15
  289.3 51.1 all-reduce.17
  355.3 51.1 all-reduce.19
  421.9 35.2 reduce-scatter.12
  460.2 86.1 all-reduce.21
  549.8 45.1 reduce-scatter.8
  598.1 51.1 reduce-scatter.14
  652.7 51.1 reduce-scatter.10
where the time goes:
time: 721 us; the launch traced here: 713 us
  waiting for transfers between devices  471 us (65%)
  matrix products  78.9 us (11%)
  other arithmetic  62.7 us (9%)
  local copies, waits for them, and re-layouts  58.7 us (8%)
  blocking collectives  24.5 us (3%)
  between operations  15.4 us (2%)
    psum x4, waiting for transfers between devices, branch_total(): lax.psum(partial_value.astype(jnp.bfloat16), 'tensor').astype(jnp.float32)  208 us
    psum x3, waiting for transfers between devices, input_total(): lax.psum(partial_value.astype(jnp.bfloat16), 'tensor').astype(jnp.float32)  147 us
    unnamed x13, waiting for transfers between devices  52.6 us
    reduce_scatter x1, waiting for transfers between devices, on_device(): lax.psum_scatter(up_all.astype(jnp.bfloat16), 'dp', scatter_dimension=1,...  51.5 us
    unnamed x150, local copies, waits for them, and re-layouts  47.4 us
    psum x1, blocking collectives, on_device(): lax.psum(gain_grads.astype(jnp.bfloat16), 'dp').astype(jnp.float32)  24.5 us
    reduce_sum x12, other arithmetic, layer_norm(): return centered * lax.rsqrt(variance + NORM_EPS) * gain_vec + shift_vec  19.1 us
  transfers between devices with their start and end apart: 11, of which 10 were waited for; matrix products, arithmetic and copies ran while one was open for 13% of the time, Pallas kernels for 0%

commit v1 on v0

--- a/solution.py
+++ b/solution.py
@@ -64,7 +64,9 @@
     slopes = jnp.exp2(-8.0 * head_index.astype(f32) / HEADS)
 
     def branch_total(partial_value):
-        return lax.psum(partial_value.astype(jnp.bfloat16), "tensor").astype(jnp.float32)
+        return jnp.sum(lax.all_gather(partial_value.astype(jnp.bfloat16), "tensor"), axis=0).astype(
+            jnp.float32
+        )
 
     def input_total(partial_value):
         return lax.psum(partial_value.astype(jnp.bfloat16), "tensor").astype(jnp.float32)

time: 721 us -> 869 us (1.21)
  waiting for transfers between devices: 471 us -> 617 us
  matrix products: 78.9 us -> 66.8 us
  other arithmetic: 62.7 us -> 73.4 us
    all_gather x0 -> x4, waiting for transfers between devices: none -> 318 us  [branch_total(): lax.all_gather(partial_value.astype(jnp.bfloat16), 'tensor')]
    psum x4 -> x0, waiting for transfers between devices: 208 us -> none  [branch_total(): lax.psum(partial_value.astype(jnp.bfloat16), 'tensor').astype(jnp.float32)]
    reduce_scatter x1, waiting for transfers between devices: 11.8 us -> 47.5 us  [on_device(): lax.psum_scatter(qkv_all.astype(jnp.bfloat16), 'dp', scatter_dimension=1,...]
    reduce_sum x0 -> x4, other arithmetic: none -> 16.5 us  [branch_total(): jnp.sum(lax.all_gather(partial_value.astype(jnp.bfloat16), 'tensor'), axi...]
    unnamed x150 -> x160, local copies, waits for them, and re-layouts: 47.4 us -> 48.9 us
    psum x3 -> x4, waiting for transfers between devices: 147 us -> 147 us  [input_total(): lax.psum(partial_value.astype(jnp.bfloat16), 'tensor').astype(jnp.float32)]
    unnamed x13 -> x14, waiting for transfers between devices: 52.6 us -> 52.8 us
  transfers between devices with their start and end apart: 11 -> 12, of which waited for: 10 -> 10; matrix products, arithmetic and copies ran while one was open for 13% -> 9% of each run, Pallas kernels for 0% -> 0%
where the time goes in v1:
time: 869 us; the launch traced here: 860 us
  waiting for transfers between devices  617 us (71%)
  other arithmetic  73.4 us (8%)
  matrix products  66.8 us (8%)
  local copies, waits for them, and re-layouts  60.9 us (7%)
  blocking collectives  24.7 us (3%)
  between operations  15.6 us (2%)
    all_gather x4, waiting for transfers between devices, branch_total(): lax.all_gather(partial_value.astype(jnp.bfloat16), 'tensor')  318 us
    psum x4, waiting for transfers between devices, input_total(): lax.psum(partial_value.astype(jnp.bfloat16), 'tensor').astype(jnp.float32)  147 us
    unnamed x14, waiting for transfers between devices  52.8 us
    reduce_scatter x1, waiting for transfers between devices, on_device(): lax.psum_scatter(up_all.astype(jnp.bfloat16), 'dp', scatter_dimension=1,...  51.3 us
    unnamed x160, local copies, waits for them, and re-layouts  48.9 us
    reduce_scatter x1, waiting for transfers between devices, on_device(): lax.psum_scatter(qkv_all.astype(jnp.bfloat16), 'dp', scatter_dimension=1,...  47.5 us
    psum x1, blocking collectives, on_device(): lax.psum(gain_grads.astype(jnp.bfloat16), 'dp').astype(jnp.float32)  24.7 us
  transfers between devices with their start and end apart: 12, of which 10 were waited for; matrix products, arithmetic and copies ran while one was open for 9% of the time, Pallas kernels for 0%

profile of v1, /device:TPU:0, one launch (start us, length us, event | category | flops | bytes accessed | tf_op | source)
XLA Modules:
  0.0 860.1 jit_solution(16740213471466628782)
XLA Ops:
  20.0 83.5 %all-gather.9.cloned.1.call-done = bf16[2048,1024]{1,0:T(8,128)(2,1)} async-done(((bf16[512,1024]{1,0:T(8,128)(2,1)}), bf16[2048,1024]{1,0:T(8,128)(2,1)}) %all-gather.9.cloned.1.call-update) | async-done | bytes 4194320 | tf_op jit(solution)/shard_map/all_gather | solution.py:67
  103.5 3.3 reduce_sum.386
  115.5 78.6 %all-gather.11.cloned.1.call-done = bf16[2048,1024]{1,0:T(8,128)(2,1)} async-done(((bf16[512,1024]{1,0:T(8,128)(2,1)}), bf16[2048,1024]{1,0:T(8,128)(2,1)}) %all-gather.11.cloned.1.call-update) | async-done | bytes 4194320 | tf_op jit(solution)/shard_map/all_gather | solution.py:67
  194.1 4.4 reduce_sum.392
  212.0 77.9 %all-gather.13.cloned.1.call-done = bf16[2048,1024]{1,0:T(8,128)(2,1)} async-done(((bf16[512,1024]{1,0:T(8,128)(2,1)}), bf16[2048,1024]{1,0:T(8,128)(2,1)}) %all-gather.13.cloned.1.call-update) | async-done | bytes 4194320 | tf_op jit(solution)/shard_map/all_gather | solution.py:67
  289.9 4.4 reduce_sum.399
  299.7 3.5 fusion.155
  306.5 4.7 fusion.83
  311.5 45.5 %all-reduce.6.cloned.1.call-done = bf16[512,1024]{1,0:T(8,128)(2,1)} async-done(((bf16[512,1024]{1,0:T(8,128)(2,1)}), bf16[512,1024]{1,0:T(8,128)(2,1)}) %all-reduce.6.cloned.1.call-update) | async-done | bytes 1048592 | tf_op jit(solution)/shard_map/psum | solution.py:72
  360.9 78.1 %all-gather.15.cloned.1.call-done = bf16[2048,1024]{1,0:T(8,128)(2,1)} async-done(((bf16[512,1024]{1,0:T(8,128)(2,1)}), bf16[2048,1024]{1,0:T(8,128)(2,1)}) %all-gather.15.cloned.1.call-update) | async-done | bytes 4194320 | tf_op jit(solution)/shard_map/all_gather | solution.py:67
  439.0 4.4 reduce_sum.405
  443.4 4.0 fusion.144
  461.1 3.6 bitcast_convert_fusion.1
  464.9 50.5 %all-reduce.8.cloned.1.call-done = bf16[512,1024]{1,0:T(8,128)(2,1)} async-done(((bf16[512,1024]{1,0:T(8,128)(2,1)}), bf16[512,1024]{1,0:T(8,128)(2,1)}) %all-reduce.8.cloned.1.call-update) | async-done | bytes 1048592 | tf_op jit(solution)/shard_map/psum | solution.py:72
  529.2 50.8 %all-reduce.10.cloned.1.call-done = bf16[512,1024]{1,0:T(8,128)(2,1)} async-done(((bf16[512,1024]{1,0:T(8,128)(2,1)}), bf16[512,1024]{1,0:T(8,128)(2,1)}) %all-reduce.10.cloned.1.call-update) | async-done | bytes 1048592 | tf_op jit(solution)/shard_map/psum | solution.py:72
  599.2 3.6 bitcast_convert_fusion
  606.8 3.7 copy.97
  618.9 3.8 convert_bitcast_fusion
  626.7 11.4 %copy.99 = bf16[2,1024,1024]{1,0,2:T(2,128)(2,1)} copy(bf16[2,1024,1024]{2,1,0:T(8,128)(2,1)} %pad_maximum_fusion.1) | data formatting | bytes 8388608
  638.1 5.6 copy.104
  661.6 24.7 %all-reduce = (bf16[2,2,1024]{2,1,0:T(2,128)(2,1)S(1)}, bf16[2,2,1024]{2,1,0:T(2,128)(2,1)S(1)}, bf16[2,2,256]{2,1,0:T(2,128)(2,1)S(1)}, bf16[2,2,1024]{2,1,0:T(2,128)(2,1)S(1)}, bf16[2,1024]{1,0:T(2,128)(2,1)S(1)}) all-reduce(bf16[2,2,1024]{2,1,0:T(2,128)(2,1)S(1)} %pad_maximum_fusion.6, ...), channel_id=1, replica_groups=mesh['dp'=8,'tensor'=4] {'dp'}, use_global_device_ids=true, to_apply=%region_36.37 | all-reduce | flops 15360 | bytes 61440 | tf_op jit(solution)/shard_map/psum | solution.py:219
  694.5 47.5 %reduce-scatter.9.cloned.1.call-done = bf16[2,128,3,256]{3,1,2,0:T(8,128)(2,1)} async-done(((bf16[2,1024,3,256]{3,1,2,0:T(8,128)(2,1)}), bf16[2,128,3,256]{3,1,2,0:T(8,128)(2,1)}) %reduce-scatter.9.cloned.1.call-update) | async-done | bytes 393232 | tf_op jit(solution)/shard_map/reduce_scatter | solution.py:230
  743.9 52.6 %reduce-scatter.15.cloned.1.call-done = bf16[128,2048]{1,0:T(8,128)(2,1)} async-done(((bf16[1024,2048]{1,0:T(8,128)(2,1)}), bf16[128,2048]{1,0:T(8,128)(2,1)}) %reduce-scatter.15.cloned.1.call-update) | async-done | bytes 524304
  799.5 51.3 %reduce-scatter.11.cloned.1.call-done = bf16[2,128,1024]{2,1,0:T(8,128)(2,1)} async-done(((bf16[2,1024,1024]{2,1,0:T(8,128)(2,1)}), bf16[2,128,1024]{2,1,0:T(8,128)(2,1)}) %reduce-scatter.11.cloned.1.call-update) | async-done | bytes 524304 | tf_op jit(solution)/shard_map/reduce_scatter | solution.py:236
  (324 shorter events, 143.0 us)
Async XLA Ops:
  7.2 96.3 %all-gather.9.cloned.1.call-start = ((), (), s32[]{:S(2)}) async-start(), calls=%async_computation.10 | async-start | bytes 5242880 | tf_op jit(solution)/shard_map/all_gather | solution.py:67
  7.4 6.4 copy-start.44
  9.8 191.3 %copy-start.58 = (f32[1,1,1024]{2,1,0:T(1,128)}, f32[1,1,1024]{2,1,0:T(1,128)S(1)}, u32[]{:S(2)}) copy-start(f32[1,1,1024]{2,1,0:T(1,128)S(1)} %get-tuple-element.55) | copy-start | bytes 12292
  19.9 174.2 %all-gather.11.cloned.1.call-start = ((), (), s32[]{:S(2)}) async-start(), calls=%async_computation.11 | async-start | bytes 5242880 | tf_op jit(solution)/shard_map/all_gather | solution.py:67
  114.7 175.2 %all-gather.13.cloned.1.call-start = ((), (), s32[]{:S(2)}) async-start(), calls=%async_computation.12 | async-start | bytes 5242880 | tf_op jit(solution)/shard_map/all_gather | solution.py:67
  202.6 3.7 copy-start.28
  210.5 146.5 %all-reduce.6.cloned.1.call-start = ((), (), s32[]{:S(2)}) async-start(), calls=%async_computation.4 | async-start | bytes 2097152 | tf_op jit(solution)/shard_map/psum | solution.py:72
  298.2 5.0 copy-start.73
  306.5 132.6 %all-gather.15.cloned.1.call-start = ((), (), s32[]{:S(2)}) async-start(), calls=%async_computation.13 | async-start | bytes 5242880 | tf_op jit(solution)/shard_map/all_gather | solution.py:67
  311.2 204.1 %all-reduce.8.cloned.1.call-start = ((), (), s32[]{:S(2)}) async-start(), calls=%async_computation.5 | async-start | bytes 2097152 | tf_op jit(solution)/shard_map/psum | solution.py:72
  443.4 5.4 copy-start.32
  443.4 5.9 copy-start.4
  464.8 115.2 %all-reduce.10.cloned.1.call-start = ((), (), s32[]{:S(2)}) async-start(), calls=%async_computation.6 | async-start | bytes 2097152 | tf_op jit(solution)/shard_map/psum | solution.py:72
  519.5 5.9 copy-start.23
  522.4 4.1 copy-start.66
  528.7 128.2 %all-reduce.12.cloned.1.call-start = ((), (), s32[]{:S(2)}) async-start(), calls=%async_computation.7 | async-start | bytes 2097152 | tf_op jit(solution)/shard_map/psum | solution.py:72
  585.1 3.7 copy-start.11
  602.8 89.8 %reduce-scatter.13.cloned.1.call-start = ((), (), s32[]{:S(2)}) async-start(), calls=%async_computation.14 | async-start | bytes 1179648
  612.9 129.0 %reduce-scatter.9.cloned.1.call-start = ((), (), s32[]{:S(2)}) async-start(), calls=%async_computation.8 | async-start | bytes 3538944 | tf_op jit(solution)/shard_map/reduce_scatter | solution.py:230
  618.6 4.1 copy-start.25
  618.6 177.9 %reduce-scatter.15.cloned.1.call-start = ((), (), s32[]{:S(2)}) async-start(), calls=%async_computation.15 | async-start | bytes 4718592
  618.9 3.9 copy-start.71
  643.7 207.2 %reduce-scatter.11.cloned.1.call-start = ((), (), s32[]{:S(2)}) async-start(), calls=%async_computation.9 | async-start | bytes 4718592 | tf_op jit(solution)/shard_map/reduce_scatter | solution.py:236
  658.4 31.0 %copy-start.13 = (f32[512,1024]{1,0:T(8,128)S(1)}, f32[512,1024]{1,0:T(8,128)}, u32[]{:S(2)}) copy-start(f32[512,1024]{1,0:T(8,128)} %copy-done.11) | copy-start | bytes 6291460
  (64 other events, 128.3 us)
Sparse Core Ops, SparseCore 0:
  20.0 83.4 all-gather.8
  114.8 79.2 all-gather.10
  210.7 79.2 all-gather.12
  306.6 50.3 all-reduce.5
  359.0 79.9 all-gather.14
  464.9 50.3 all-reduce.7
  528.9 51.1 all-reduce.9
  603.0 51.1 all-reduce.11
  657.3 35.3 reduce-scatter.12
  695.9 46.0 reduce-scatter.8
  745.3 51.1 reduce-scatter.14
  799.7 51.0 reduce-scatter.10
